TPU v7x, 32 devices: a whole 2x2x4 slice. The times are simulated.
32 devices in a mesh: fsdp: 16 (over z, y, core), tp: 2 (over x).
Axes of the slice: x: 2, y: 2, z: 4, core: 2. Of those that a mesh axis runs over, the one named last changes fastest.
Arguments:
- grad_query: bfloat16 [2, 16, 2560, 768], P(None, 'fsdp', None, 'tp'), as said below
- grad_latent: bfloat16 [2, 16, 2560, 288], P(None, 'fsdp', None, 'tp'), as said below
- grad_gains: bfloat16 [2, 16, 1024], P(None, 'fsdp'), as said below
- param_query: float32 [2560, 768], P('fsdp', 'tp'), may hold values from -0.125 to 0.125
- param_latent: float32 [2560, 288], P('fsdp', 'tp'), may hold values from -0.125 to 0.125
- param_gains: float32 [1024], P('fsdp'), may hold values from -0.125 to 0.125
- first_query: float32 [2560, 768], P('fsdp', 'tp'), may hold values from -4 to 4
- first_latent: float32 [2560, 288], P('fsdp', 'tp'), may hold values from -4 to 4
- first_gains: float32 [1024], P('fsdp'), may hold values from -4 to 4
- second_query: float32 [2560, 768], P('fsdp', 'tp'), may hold values from 0.05 to 2
- second_latent: float32 [2560, 288], P('fsdp', 'tp'), may hold values from 0.05 to 2
- second_gains: float32 [1024], P('fsdp'), may hold values from 0.05 to 2
Outputs:
- new_query: float32 [2560, 768], P('fsdp', 'tp')
- new_latent: float32 [2560, 288], P('fsdp', 'tp')
- new_gains: float32 [1024], P('fsdp')
- next_first_query: float32 [2560, 768], P('fsdp', 'tp')
- next_first_latent: float32 [2560, 288], P('fsdp', 'tp')
- next_first_gains: float32 [1024], P('fsdp')
- next_second_query: float32 [2560, 768], P('fsdp', 'tp')
- next_second_latent: float32 [2560, 288], P('fsdp', 'tp')
- next_second_gains: float32 [1024], P('fsdp')
- train_query: bfloat16 [2560, 768], P(None, 'tp')
- train_latent: bfloat16 [2560, 288], P(None, 'tp')
- train_gains: bfloat16 [1024], replicated
Inputs may be any that keep to these rules, and one draw needn't show every extreme that they name: `grad_query`: each device's gradient of its own tokens. `grad_latent`: each device's gradient of its own tokens. `grad_gains`: each device's gradient of its own tokens.
All inputs are finite; a program needn't handle non-finite values.
Results may differ from a plain program's by a relative error of at most 0.0004.
Values may be sent and summed in bfloat16 or wider, within the bound.
A program may use at most 64 MiB of HBM per device.

v0:
```python
import jax
import jax.numpy as jnp
from jax import lax
from jax.sharding import PartitionSpec as P

D = 2560
QR = 768
STEP = 10
KVA = 288
GAINS = 1024


beta_first = 0.9
beta_second = 0.95
rate = 0.01


def adamw(gradient, weights, first, second, factor, decay):
    scaled = factor * gradient
    first_new = beta_first * first + (1.0 - beta_first) * scaled
    second_new = beta_second * second + (1.0 - beta_second) * scaled * scaled
    ratio = (
        first_new
        / (1.0 - beta_first**STEP)
        / (jnp.sqrt(second_new / (1.0 - beta_second**STEP)) + 1e-08)
    )
    weights_new = weights - rate * (ratio + decay * weights)
    return (weights_new, first_new, second_new)


def local(
    grad_query,
    grad_latent,
    grad_gains,
    param_query,
    param_latent,
    param_gains,
    first_query,
    first_latent,
    first_gains,
    second_query,
    second_latent,
    second_gains,
):
    tp_count = lax.axis_size("tp")
    totals = None
    for micro_index in range(grad_query.shape[0]):
        pieces = (
            lax.psum_scatter(
                grad_query[micro_index, 0].astype(jnp.float32),
                "fsdp",
                scatter_dimension=0,
                tiled=True,
            ),
            lax.psum_scatter(
                grad_latent[micro_index, 0].astype(jnp.float32),
                "fsdp",
                scatter_dimension=0,
                tiled=True,
            ),
            lax.psum_scatter(
                grad_gains[micro_index, 0].astype(jnp.float32),
                "fsdp",
                scatter_dimension=0,
                tiled=True,
            ),
        )
        if totals is None:
            totals = pieces
        else:
            totals = (totals[0] + pieces[0], totals[1] + pieces[1], totals[2] + pieces[2])
    sum_query = 0.5 * totals[0]
    sum_latent = 0.5 * totals[1]
    sum_gains = 0.5 * totals[2]
    local_squares = (
        jnp.sum(sum_query * sum_query)
        + jnp.sum(sum_latent * sum_latent)
        + jnp.sum(sum_gains * sum_gains) / tp_count
    )
    squares = lax.psum(local_squares, ("fsdp", "tp"))
    count = D * (QR + KVA) + GAINS
    rms_value = jnp.sqrt(squares / count + 1e-06)
    factor = jnp.minimum(jnp.float32(1.0), 1.0 / rms_value)
    new_query, next_first_query, next_second_query = adamw(
        sum_query, param_query, first_query, second_query, factor, 0.1
    )
    new_latent, next_first_latent, next_second_latent = adamw(
        sum_latent, param_latent, first_latent, second_latent, factor, 0.1
    )
    new_gains, next_first_gains, next_second_gains = adamw(
        sum_gains, param_gains, first_gains, second_gains, factor, 0.0
    )
    train_query, train_latent, train_gains = (
        lax.all_gather(new_query.astype(jnp.bfloat16), "fsdp", axis=0, tiled=True),
        lax.all_gather(new_latent.astype(jnp.bfloat16), "fsdp", axis=0, tiled=True),
        lax.all_gather(new_gains.astype(jnp.bfloat16), "fsdp", axis=0, tiled=True),
    )
    return (
        new_query,
        new_latent,
        new_gains,
        next_first_query,
        next_first_latent,
        next_first_gains,
        next_second_query,
        next_second_latent,
        next_second_gains,
        train_query,
        train_latent,
        train_gains,
    )


def solution(mesh):
    in_specs = (
        P(None, "fsdp", None, "tp"),
        P(None, "fsdp", None, "tp"),
        P(None, "fsdp", None),
        P("fsdp", "tp"),
        P("fsdp", "tp"),
        P("fsdp"),
        P("fsdp", "tp"),
        P("fsdp", "tp"),
        P("fsdp"),
        P("fsdp", "tp"),
        P("fsdp", "tp"),
        P("fsdp"),
    )
    out_specs = (
        P("fsdp", "tp"),
        P("fsdp", "tp"),
        P("fsdp"),
        P("fsdp", "tp"),
        P("fsdp", "tp"),
        P("fsdp"),
        P("fsdp", "tp"),
        P("fsdp", "tp"),
        P("fsdp"),
        P(None, "tp"),
        P(None, "tp"),
        P(),
    )
    return jax.shard_map(local, mesh=mesh, in_specs=in_specs, out_specs=out_specs, check_vma=False)
```

profile of v0, /device:TPU:0, one launch (start us, length us, event | category | flops | bytes accessed | tf_op | source)
XLA Modules:
  0.0 268.9 jit_solution(12875552986359171967)
XLA Ops:
  7.2 1.5 add_bitcast_fusion.1
  8.8 2.1 copy.26
  10.8 0.0 reduce-scatter.5.cloned.1.call-start
  10.9 4.4 %add_bitcast_fusion = f32[2560,384]{1,0:T(8,128)} fusion(bf16[2,1,2560,384]{3,2,1,0:T(8,128)(2,1)} %param.12), kind=kLoop, calls=%fused_computation | loop fusion | flops 2949120 | bytes 7864320 | tf_op jit(solution)/shard_map/add | solution.py:71
  15.4 0.0 all-gather.3.cloned.1.call-start
  15.4 0.5 copy-done.7
  15.9 0.6 fusion.8
  17.2 35.1 %all-reduce.1 = f32[1024]{0:T(1024)S(1)} all-reduce(f32[1024]{0:T(1024)S(1)} %bitcast.12), channel_id=7, replica_groups=mesh['fsdp'=16,'tp'=2] {'fsdp'}, use_global_device_ids=true, to_apply=%region_6.0.clone | all-reduce | flops 1024 | bytes 8192
  52.3 0.7 multiply_reduce_fusion.2
  53.7 24.8 %reduce-scatter.7.cloned.1.call-done = f32[160,144]{1,0:T(8,128)} async-done(((f32[2560,144]{1,0:T(8,128)}), f32[160,144]{1,0:T(8,128)}) %reduce-scatter.7.cloned.1.call-update) | async-done | bytes 92176
  78.5 1.0 copy.27
  79.5 0.6 multiply_reduce_fusion.1
  80.1 71.7 %reduce-scatter.5.cloned.1.call-done = f32[160,384]{1,0:T(8,128)} async-done(((f32[2560,384]{1,0:T(8,128)}), f32[160,384]{1,0:T(8,128)}) %reduce-scatter.5.cloned.1.call-update) | async-done | bytes 245776 | tf_op jit(solution)/shard_map/reduce_scatter | solution.py:49
  151.8 1.6 multiply_reduce_fusion
  154.7 39.6 %psum.7 = f32[]{:T(128)} all-reduce(f32[]{:T(128)S(6)} %add.81), channel_id=1, replica_groups=mesh['fsdp'=16,'tp'=2] {'fsdp','tp'}, use_global_device_ids=true, to_apply=%region_9.0 | all-reduce | flops 1 | bytes 8 | tf_op jit(solution)/shard_map/psum | solution.py:80
  195.0 2.0 fusion.6
  197.7 0.8 convert_bitcast_fusion
  198.5 24.8 %all-gather = bf16[16,160,144]{1,2,0:T(8,128)(2,1)S(1)} all-gather(bf16[1,160,144]{1,2,0:T(8,128)(2,1)S(1)} %get-tuple-element.16), channel_id=1, replica_groups=mesh['fsdp'=16,'tp'=2] {'fsdp'}, dimensions={0}, use_global_device_ids=true | all-gather | bytes 783360 | tf_op jit(solution)/shard_map/all_gather | solution.py:95
  223.3 0.4 copy.25
  223.7 2.8 %reshape.49 = bf16[2560,144]{0,1:T(8,128)(2,1)} reshape(bf16[16,160,144]{1,0,2:T(8,128)(2,1)S(1)} %copy.25) | data formatting | bytes 1474560
  226.5 0.6 fusion.3
  227.1 0.2 dynamic-update-slice
  227.3 32.1 %all-reduce = bf16[1024]{0:T(1024)(128)(2,1)} all-reduce(bf16[1024]{0:T(1024)(128)(2,1)S(1)} %dynamic-update-slice), channel_id=1, replica_groups=mesh['fsdp'=16,'tp'=2] {'fsdp'}, use_global_device_ids=true, to_apply=%add | all-reduce | flops 1024 | bytes 4096
  259.3 3.0 %copy.30 = bf16[2560,384]{1,0:T(8,128)(2,1)} copy(bf16[2560,384]{1,0:T(8,128)(2,1)} %all-gather.3.cloned.1.call-done) | data formatting | bytes 3932160
  (28 shorter events, 0.2 us)
Async XLA Ops:
  7.2 71.3 %reduce-scatter.7.cloned.1.call-start = ((), (), s32[]{:S(2)}) async-start(), calls=%async_computation.4 | async-start | bytes 2785280
  10.8 141.0 %reduce-scatter.5.cloned.1.call-start = ((), (), s32[]{:S(2)}) async-start(), calls=%async_computation.3 | async-start | bytes 4177920 | tf_op jit(solution)/shard_map/reduce_scatter | solution.py:49
  15.3 0.7 copy-start.7
  15.3 1.9 copy-start.6
  15.3 179.7 %copy-start = (f32[160,384]{1,0:T(8,128)S(1)}, f32[160,384]{1,0:T(8,128)}, u32[]{:S(2)}) copy-start(f32[160,384]{1,0:T(8,128)} %param.15) | copy-start | bytes 737284
  15.3 179.7 %copy-start.1 = (f32[160,384]{1,0:T(8,128)S(1)}, f32[160,384]{1,0:T(8,128)}, u32[]{:S(2)}) copy-start(f32[160,384]{1,0:T(8,128)} %param.18) | copy-start | bytes 737284
  15.3 179.7 %copy-start.2 = (f32[160,384]{1,0:T(8,128)S(1)}, f32[160,384]{1,0:T(8,128)}, u32[]{:S(2)}) copy-start(f32[160,384]{1,0:T(8,128)} %param.21) | copy-start | bytes 737284
  15.3 182.3 %copy-start.3 = (f32[160,144]{0,1:T(8,128)S(1)}, f32[160,144]{0,1:T(8,128)}, u32[]{:S(2)}) copy-start(f32[160,144]{0,1:T(8,128)} %param.16) | copy-start | bytes 276484
  15.3 182.3 %copy-start.4 = (f32[160,144]{0,1:T(8,128)S(1)}, f32[160,144]{0,1:T(8,128)}, u32[]{:S(2)}) copy-start(f32[160,144]{0,1:T(8,128)} %param.19) | copy-start | bytes 276484
  15.4 182.3 %copy-start.5 = (f32[160,144]{0,1:T(8,128)S(1)}, f32[160,144]{0,1:T(8,128)}, u32[]{:S(2)}) copy-start(f32[160,144]{0,1:T(8,128)} %param.22) | copy-start | bytes 276484
  15.4 244.0 %all-gather.3.cloned.1.call-start = ((), (), s32[]{:S(2)}) async-start(), calls=%async_computation.2 | async-start | bytes 2088960 | tf_op jit(solution)/shard_map/all_gather | solution.py:94
  223.3 3.2 %copy-start.8 = (f32[64]{0:T(128)S(1)}, f32[64]{0:T(128)}, u32[]{:S(2)}) copy-start(f32[64]{0:T(128)} %param.17) | copy-start | bytes 772
  223.3 3.2 %copy-start.9 = (f32[64]{0:T(128)S(1)}, f32[64]{0:T(128)}, u32[]{:S(2)}) copy-start(f32[64]{0:T(128)} %param.20) | copy-start | bytes 772
  223.3 3.2 %copy-start.10 = (f32[64]{0:T(128)S(1)}, f32[64]{0:T(128)}, u32[]{:S(2)}) copy-start(f32[64]{0:T(128)} %param.23) | copy-start | bytes 772
Sparse Core Ops, SparseCore 0:
  11.8 66.6 reduce-scatter.6
  82.4 69.4 reduce-scatter.4
  197.1 42.7 all-gather.2
where the time goes:
time: 269 us
  blocking collectives  132 us (49%)
  waiting for transfers between devices  96.5 us (36%)
  between operations  17.8 us (7%)
  other arithmetic  12.3 us (5%)
  local copies, waits for them, and re-layouts  10.6 us (4%)
    reduce_scatter x1, waiting for transfers between devices, local(): lax.psum_scatter(grad_query[micro_index, 0].astype(jnp.float32), 'fsdp',...  71.7 us
    unnamed x2, blocking collectives  67.2 us
    psum x1, blocking collectives, local(): squares = lax.psum(local_squares, ('fsdp', 'tp'))  39.6 us
    unnamed x4, waiting for transfers between devices  24.8 us
    all_gather x1, blocking collectives, local(): lax.all_gather(new_latent.astype(jnp.bfloat16), 'fsdp', axis=0, tiled=True)  24.8 us
    unnamed x29, local copies, waits for them, and re-layouts  10.2 us
  transfers between devices with their start and end apart: 3, of which 2 were waited for; matrix products, arithmetic and copies ran while one was open for 5% of the time, Pallas kernels for 0%

commit v1 on v0

v1 whole, which is shorter than its diff:
```python
import functools

import jax
import jax.numpy as jnp
from jax import lax
from jax.experimental import pallas as pl
from jax.experimental.pallas import tpu as pltpu
from jax.sharding import PartitionSpec as P

STEP = 10

beta_first = 0.9
beta_second = 0.95
rate = 0.01

LANES = 128
MESH = pl.DeviceIdType.MESH
f32 = jnp.float32
bf16 = jnp.bfloat16


class Plan:
    def __init__(self, n, tp, mb, own_rows, wq, wl, gains):
        self.n, self.tp, self.mb, self.own_rows = n, tp, mb, own_rows
        self.m = n // 2
        self.bits = self.m.bit_length() - 1
        self.rp = -(-own_rows // 16) * 16
        self.wq, self.wl, self.gn = wq, wl, gains // n
        self.nq, self.nl, self.left = wq // LANES, wl // LANES, wl % LANES
        self.slots = LANES // self.left
        self.groups = self.rp // 16
        self.main = self.rp * (self.nq + self.nl)
        self.grow = self.main + 16 * (self.groups // self.slots)
        self.rows = self.grow + 16
        self.glane = 64
        assert wq % LANES == 0 and LANES % self.left == 0 and self.gn <= 64
        assert self.groups % self.slots * self.left <= self.glane
        assert 2 << self.bits == n
        self.cut = int(self.rows * 0.5) // 16 * 16
        self.halves = ((0, self.cut), (self.cut, self.rows - self.cut))
        first = list(range(self.bits))
        second = first[1:2] + first[:1] + first[2:]
        self.orders = (first, second)

    def leftover(self):
        for g in range(self.groups):
            yield self.main + 16 * (g // self.slots), self.left * (g % self.slots), 16 * g

    def slots_after(self, half, step):
        done = self.orders[half][: step + 1]
        return [d for d in range(self.m) if all(not d >> k & 1 for k in done)]

    def message(self, half, step, slot):
        base = half * (self.m - 1)
        for s in range(step):
            base += len(self.slots_after(half, s))
        return base + self.slots_after(half, step).index(slot)


def kernel(plan, count, *refs):
    (gq, gl, gg, pq, pl_, pg, fq, fl, fg, sq, sl, sg,
     nq, nl, ng, mq, ml, mg, vq, vl, vg, tq, tl, tg,
     own_q, own_l, in_q, in_l, in_g, gsum, acc, rbuf, total, stage, norm, ag, agc, tgs,
     cq_s, cq_r, cl_s, cl_r, cg_s, cg_r, oq, ol, rs_s, rs_r, no_s, no_r, ag_s, ag_r, ac_s, ac_r) = refs
    n, m, mb, tp, rp = plan.n, plan.m, plan.mb, plan.tp, plan.rp
    everyone = n * tp
    f, t = lax.axis_index("fsdp"), lax.axis_index("tp")
    core, up = f % 2, f // 2
    me = f * tp + t

    def flip(value, d):
        for k in range(plan.bits):
            if d >> k & 1:
                value = value + (1 << k) * (1 - 2 * (value // (1 << k) % 2))
        return value

    sibling = {"fsdp": f + 1 - 2 * core, "tp": t}

    def partner(k):
        return {"fsdp": 2 * flip(up, 1 << k) + core, "tp": t}

    def peer(i):
        other = (me + i) % everyone
        return {"fsdp": other // tp, "tp": other % tp}

    def mine(d):
        return 2 * flip(up, d) + core

    def theirs(d):
        return 2 * flip(up, d) + 1 - core

    def remote(src, dst, send, recv, to):
        return pltpu.make_async_remote_copy(
            src_ref=src, dst_ref=dst, send_sem=send, recv_sem=recv, device_id=to, device_id_type=MESH
        )

    order = sorted(range(1, m), key=lambda d: (not all(d >> o[0] & 1 for o in plan.orders),
                                               not any(d >> o[0] & 1 for o in plan.orders), d)) + [0]
    local_copies = []
    for d in order:
        a = pltpu.make_async_copy(gq.at[:, mine(d)], own_q.at[d], oq.at[d])
        b = pltpu.make_async_copy(gl.at[:, mine(d)], own_l.at[d], ol.at[d])
        a.start()
        b.start()
        local_copies.append((a, b))

    barrier = pltpu.get_barrier_semaphore()

    @pl.loop(1, everyone)
    def _(i):
        pl.semaphore_signal(barrier, inc=1, device_id=peer(i), device_id_type=MESH)

    pl.semaphore_wait(barrier, everyone - 1)

    gain_copy = remote(gg, in_g, cg_s.at[0], cg_r.at[0], sibling)
    gain_copy.start()
    core_copies = []
    for d in order:
        a = remote(gq.at[:, theirs(d)], in_q.at[d], cq_s.at[d], cq_r.at[d], sibling)
        b = remote(gl.at[:, theirs(d)], in_l.at[d], cl_s.at[d], cl_r.at[d], sibling)
        a.start()
        b.start()
        core_copies.append((a, b))

    def rs_copy(half, step, d):
        k = plan.orders[half][step]
        slot = d ^ (1 << k)
        index = plan.message(half, step, slot)
        lo, size = plan.halves[half]
        return remote(
            acc.at[d, pl.ds(lo, size)],
            rbuf.at[index, pl.ds(0, size)],
            rs_s.at[index],
            rs_r.at[index],
            partner(k),
        )

    def gather_sum(refs_, d, lo, hi):
        value = None
        for ref in refs_:
            for i in range(mb):
                term = ref[d, i, :, lo:hi].astype(f32)
                value = term if value is None else value + term
        return value

    gain_copy.wait()
    total_gains = None
    for ref in (gg, in_g):
        for i in range(mb):
            term = ref[i].astype(f32)
            total_gains = term if total_gains is None else total_gains + term
    gsum[...] = total_gains

    for place, d in enumerate(order):
        for copy in local_copies[place]:
            copy.wait()
        for copy in core_copies[place]:
            copy.wait()
        for j in range(plan.nq):
            acc[d, rp * j : rp * (j + 1)] = gather_sum((own_q, in_q), d, LANES * j, LANES * (j + 1))
        for j in range(plan.nl):
            lo = rp * (plan.nq + j)
            acc[d, lo : lo + rp] = gather_sum((own_l, in_l), d, LANES * j, LANES * (j + 1))
        acc[d, plan.main : plan.rows] = jnp.zeros((plan.rows - plan.main, LANES), f32)
        last = gather_sum((own_l, in_l), d, LANES * plan.nl, plan.wl)
        for row, lane, source in plan.leftover():
            acc[d, row : row + 16, lane : lane + plan.left] = last[source : source + 16]
        acc[d, plan.grow : plan.grow + 1, plan.glane : plan.glane + plan.gn] = gsum[pl.ds(mine(d), 1), :]
        for half in range(2):
            if d >> plan.orders[half][0] & 1:
                rs_copy(half, 0, d).start()

    def add_arrived(half, step, d):
        index = plan.message(half, step, d)
        lo, size = plan.halves[half]
        rs_copy(half, step, d ^ (1 << plan.orders[half][step])).wait_recv()
        acc[d, lo : lo + size] += rbuf[index, 0:size]

    for step in range(1, plan.bits):
        for half in range(2):
            k = plan.orders[half][step]
            for d in plan.slots_after(half, step - 1):
                if d >> k & 1:
                    for earlier in range(step):
                        add_arrived(half, earlier, d)
                    rs_copy(half, step, d).start()
    for step in range(plan.bits):
        for half in range(2):
            add_arrived(half, step, 0)

    summed = 0.5 * acc[0]
    total[...] = summed
    tail = summed[plan.main :]
    is_gain = (lax.broadcasted_iota(jnp.int32, tail.shape, 0) >= plan.grow - plan.main) & (
        lax.broadcasted_iota(jnp.int32, tail.shape, 1) >= plan.glane
    )
    tail_squares = jnp.where(is_gain, 1.0 / tp, 1.0) * tail * tail
    head = summed[: plan.main]
    squares = jnp.sum((head * head).reshape(-1, 8, LANES), axis=0)
    norm[0] = squares + jnp.sum(tail_squares.reshape(-1, 8, LANES), axis=0)

    def norm_copy(i):
        return remote(norm.at[0], norm.at[i], no_s.at[i], no_r.at[i], peer(i))

    @pl.loop(1, everyone)
    def _(i):
        norm_copy(i).start()

    @pl.loop(1, everyone)
    def _(i):
        norm_copy(i).wait()

    sum_squares = jnp.sum(jnp.sum(norm[...], axis=0), keepdims=True)
    rms = jnp.sqrt(jnp.broadcast_to(sum_squares, (1, LANES)) / count + 1e-06)
    factor = jnp.minimum(f32(1.0), 1.0 / rms)

    def update(gradient, p, first, second, decay):
        scaled = factor[:, : gradient.shape[1]] * gradient
        first_new = beta_first * first + (1.0 - beta_first) * scaled
        second_new = beta_second * second + (1.0 - beta_second) * scaled * scaled
        ratio = (first_new / (1.0 - beta_first**STEP)) / (
            jnp.sqrt(second_new / (1.0 - beta_second**STEP)) + 1e-08
        )
        return p - rate * (ratio + decay * p), first_new, second_new

    for j in range(plan.nq + plan.nl):
        params = (pq, fq, sq) if j < plan.nq else (pl_, fl, sl)
        outs = (nq, mq, vq) if j < plan.nq else (nl, ml, vl)
        lo = LANES * (j if j < plan.nq else j - plan.nq)
        values = update(total[rp * j : rp * (j + 1)], *(ref[:, lo : lo + LANES] for ref in params), 0.1)
        for ref, value in zip(outs, values):
            ref[:, lo : lo + LANES] = value
        ag[0, rp * j : rp * (j + 1)] = values[0].astype(bf16)
    stage[...] = jnp.zeros(stage.shape, f32)
    for row, lane, source in plan.leftover():
        at = (pl.ds(source, 16), pl.ds(LANES * plan.nl, plan.left))
        values = update(total[row : row + 16, lane : lane + plan.left], pl_[at], fl[at], sl[at], 0.1)
        for ref, value in zip((nl, ml, vl), values):
            ref[at] = value
        stage[row - plan.main : row - plan.main + 16, lane : lane + plan.left] = values[0]
    gain_lanes = (slice(plan.grow, plan.grow + 1), slice(plan.glane, plan.glane + plan.gn))
    values = update(total[gain_lanes], pg[...], fg[...], sg[...], 0.0)
    for ref, value in zip((ng, mg, vg), values):
        ref[...] = value
    stage[plan.grow - plan.main : plan.grow - plan.main + 1, gain_lanes[1]] = values[0]
    ag[0, plan.main : plan.rows] = stage[...].astype(bf16)

    def ag_copy(half, step, d):
        k = plan.orders[half][step]
        source = d ^ (1 << k)
        index = plan.message(half, step, source if d >> k & 1 else d)
        lo, size = plan.halves[half]
        rows = pl.ds(lo, size)
        return remote(ag.at[d, rows], ag.at[source, rows], ag_s.at[index], ag_r.at[index], partner(k))

    def across(half, d):
        lo, size = plan.halves[half]
        rows = pl.ds(lo, size)
        index = half * m + d
        return remote(ag.at[d, rows], agc.at[d, rows], ac_s.at[index], ac_r.at[index], sibling)

    def arrived(half, step, d):
        for later in reversed(range(step)):
            ag_copy(half, later, d).start()
        across(half, d).start()

    def write(ref, d, block):
        for j in range(plan.nq):
            tq[block, :, LANES * j : LANES * (j + 1)] = ref[d, rp * j : rp * (j + 1)]
        for j in range(plan.nl):
            lo = rp * (plan.nq + j)
            tl[block, :, LANES * j : LANES * (j + 1)] = ref[d, lo : lo + rp]
        for row, lane, source in plan.leftover():
            tl[block, source : source + 16, LANES * plan.nl : plan.wl] = ref[
                d, row : row + 16, lane : lane + plan.left
            ]
        gains = ref[d, plan.grow : plan.grow + 16].astype(f32)
        tgs[pl.ds(block, 1), :] = gains[0:1, plan.glane : plan.glane + plan.gn]

    for half in range(2):
        arrived(half, plan.bits, 0)
    write(ag, 0, mine(0))
    for step in reversed(range(plan.bits)):
        for half in range(2):
            k = plan.orders[half][step]
            for d in plan.slots_after(half, step):
                new = d | (1 << k)
                ag_copy(half, step, d).wait_recv()
                arrived(half, step, new)
    for d in range(1, m):
        write(ag, d, mine(d))
    for d in range(m):
        for half in range(2):
            across(half, d).wait_recv()
        write(agc, d, theirs(d))
    tg[...] = tgs[...].astype(bf16)

    for half in range(2):
        for step in range(plan.bits):
            k = plan.orders[half][step]
            for d in plan.slots_after(half, step):
                rs_copy(half, step, d | (1 << k)).wait_send()
                ag_copy(half, step, d).wait_send()
        for d in range(m):
            across(half, d).wait_send()


def local(grad_query, grad_latent, grad_gains, *state):
    n, tp = lax.axis_size("fsdp"), lax.axis_size("tp")
    mb, _, depth, wq = grad_query.shape
    wl, gains = grad_latent.shape[3], grad_gains.shape[2]
    plan = Plan(n, tp, mb, depth // n, wq, wl, gains)
    count = depth * (wq + wl) * tp + gains
    extra = plan.rp - plan.own_rows

    def blocks(x):
        x = x.reshape(mb, n, plan.own_rows, x.shape[3])
        return jnp.pad(x, ((0, 0), (0, 0), (0, extra), (0, 0))) if extra else x

    def own(x):
        if x.ndim == 1:
            return x.reshape(1, plan.gn)
        return jnp.pad(x, ((0, extra), (0, 0))) if extra else x

    state = [own(x) for x in state]
    m, rp = plan.m, plan.rp
    vmem = pl.BlockSpec(memory_space=pltpu.VMEM)
    anywhere = pl.BlockSpec(memory_space=pl.ANY)
    shapes = [(rp, wq), (rp, wl), (1, plan.gn)] * 3
    outs = pl.pallas_call(
        functools.partial(kernel, plan, count),
        out_shape=[jax.ShapeDtypeStruct(s, f32) for s in shapes]
        + [
            jax.ShapeDtypeStruct((n, rp, wq), bf16),
            jax.ShapeDtypeStruct((n, rp, wl), bf16),
            jax.ShapeDtypeStruct((n, plan.gn), bf16),
        ],
        in_specs=[anywhere, anywhere] + [vmem] * 10,
        out_specs=[vmem] * 12,
        scratch_shapes=[
            pltpu.VMEM((m, mb, rp, wq), bf16),
            pltpu.VMEM((m, mb, rp, wl), bf16),
            pltpu.VMEM((m, mb, rp, wq), bf16),
            pltpu.VMEM((m, mb, rp, wl), bf16),
            pltpu.VMEM((mb, n, plan.gn), bf16),
            pltpu.VMEM((n, plan.gn), f32),
            pltpu.VMEM((m, plan.rows, LANES), f32),
            pltpu.VMEM((2 * (m - 1), max(s for _, s in plan.halves), LANES), f32),
            pltpu.VMEM((plan.rows, LANES), f32),
            pltpu.VMEM((plan.rows - plan.main, LANES), f32),
            pltpu.VMEM((n * tp, 8, LANES), f32),
            pltpu.VMEM((m, plan.rows, LANES), bf16),
            pltpu.VMEM((m, plan.rows, LANES), bf16),
            pltpu.VMEM((n, plan.gn), f32),
        ]
        + [
            pltpu.SemaphoreType.DMA((k,))
            for k in [m] * 4 + [1] * 2 + [m] * 2 + [2 * (m - 1)] * 2 + [n * tp] * 2 + [2 * (m - 1)] * 2 + [2 * m] * 2
        ],
        compiler_params=pltpu.CompilerParams(
            collective_id=0, has_side_effects=True, vmem_limit_bytes=52 * 1024 * 1024
        ),
    )(blocks(grad_query), blocks(grad_latent), grad_gains.reshape(mb, n, plan.gn), *state)
    result = []
    for x in outs[:9]:
        if x.shape[0] == 1:
            result.append(x.reshape(plan.gn))
        else:
            result.append(x[: plan.own_rows] if extra else x)
    for x in outs[9:11]:
        result.append(x[:, : plan.own_rows].reshape(depth, x.shape[2]))
    result.append(outs[11].reshape(gains))
    return tuple(result)


def solution(mesh):
    shards = (P("fsdp", "tp"), P("fsdp", "tp"), P("fsdp"))
    in_specs = (P(None, "fsdp", None, "tp"), P(None, "fsdp", None, "tp"), P(None, "fsdp", None)) + shards * 3
    out_specs = shards * 3 + (P(None, "tp"), P(None, "tp"), P())
    return jax.shard_map(local, mesh=mesh, in_specs=in_specs, out_specs=out_specs, check_vma=False)
```

time: 269 us -> 97 us (0.36)
  blocking collectives: 132 us -> 0 us
  waiting for transfers between devices: 96.5 us -> 0 us
  Pallas kernels: 0 us -> 77.7 us
  between operations: 17.8 us -> 0.73 us
  other arithmetic: 12.3 us -> 0 us
  local copies, waits for them, and re-layouts: 10.6 us -> 18 us
    pallas_call x0 -> x1, Pallas kernels: none -> 77.7 us  [local(): pl.pallas_call(functools.partial(kernel, plan, count), out_shape=[jax.Sha...]
    reduce_scatter x1 -> x0, waiting for transfers between devices: 71.7 us -> none  [local(): lax.psum_scatter(grad_query[micro_index, 0].astype(jnp.float32), 'fsdp',...]
    unnamed x2 -> x0, blocking collectives: 67.2 us -> none
    psum x1 -> x0, blocking collectives: 39.6 us -> none  [local(): squares = lax.psum(local_squares, ('fsdp', 'tp'))]
    unnamed x4 -> x0, waiting for transfers between devices: 24.8 us -> none
    all_gather x1 -> x0, blocking collectives: 24.8 us -> none  [local(): lax.all_gather(new_latent.astype(jnp.bfloat16), 'fsdp', axis=0, tiled=True)]
    unnamed x29 -> x25, local copies, waits for them, and re-layouts: 10.2 us -> 16.5 us
    add x3 -> x0, other arithmetic: 5.93 us -> none  [the longest x1 4.39 us: local(): totals[0] + pieces[0]]
  transfers between devices with their start and end apart: 3 -> 0, of which waited for: 2 -> 0; matrix products, arithmetic and copies ran while one was open for 5% -> 0% of each run, Pallas kernels for 0% -> 0%
where the time goes in v1:
time: 97 us; the launch traced here: 96.4 us
  Pallas kernels  77.7 us (80%)
  local copies, waits for them, and re-layouts  18 us (19%)
    pallas_call x1, Pallas kernels, local(): pl.pallas_call(functools.partial(kernel, plan, count), out_shape=[jax.Sha...  77.7 us
    unnamed x25, local copies, waits for them, and re-layouts  16.5 us

profile of v1, /device:TPU:0, one launch (start us, length us, event | category | flops | bytes accessed | tf_op | source)
XLA Modules:
  0.0 96.4 jit_solution(14055572362526417546)
XLA Ops:
  0.6 0.8 reshape.62.refs_2_
  1.4 1.0 %copy.25.refs_4_ = f32[160,144]{1,0:T(8,128)S(1)} copy(f32[160,144]{0,1:T(8,128)} %param.16) | data formatting | bytes 184320 | tf_op args[4]
  2.4 1.0 %copy.26.refs_7_ = f32[160,144]{1,0:T(8,128)S(1)} copy(f32[160,144]{0,1:T(8,128)} %param.19) | data formatting | bytes 184320 | tf_op args[7]
  3.5 1.0 %copy.27.refs_10_ = f32[160,144]{1,0:T(8,128)S(1)} copy(f32[160,144]{0,1:T(8,128)} %param.22) | data formatting | bytes 184320 | tf_op args[10]
  4.5 0.0 copy-start
  4.5 0.0 copy-start.1
  4.5 0.0 copy-start.2
  4.5 0.0 copy-start.3
  4.5 4.0 %copy.24 = bf16[2,1,2560,144]{3,2,0,1:T(8,128)(2,1)} copy(bf16[2,1,2560,144]{2,3,1,0:T(8,128)(2,1)} %param.13) | data formatting | bytes 2949120 | tf_op args[1]
  8.6 0.0 copy-done.2
  8.6 0.0 copy-done.3
  8.6 77.7 %shard_map.211 = (f32[160,384]{1,0:T(8,128)S(1)}, f32[160,144]{1,0:T(8,128)S(1)}, f32[1,64]{1,0:T(1,128)S(1)}, f32[160,384]{1,0:T(8,128)S(1)}, f32[160,144]{1,0:...) custom-call(bf16[2,16,160,384]{3,2,1,0:T(8,128)(2,1)} %bitcast.19, ...), custom_call_target="tpu_custom_call" | custom-call | tf_op jit(solution)/shard_map/pallas_call | solution.py:330
  86.3 0.7 reshape.71
  86.9 0.8 copy.28
  87.7 0.8 copy.29
  88.5 0.8 copy.30
  89.2 2.2 %copy.31 = bf16[2560,144]{0,1:T(8,128)(2,1)} copy(bf16[2560,144]{1,0:T(8,128)(2,1)} %bitcast.21) | data formatting | bytes 1474560
  91.5 0.7 copy.39
  92.2 0.5 copy.40
  92.7 0.7 copy.41
  93.4 0.5 copy.42
  93.9 0.7 copy.43
  94.6 0.5 copy.44
  95.1 1.3 %copy.45 = bf16[2560,384]{1,0:T(8,128)(2,1)} copy(bf16[2560,384]{1,0:T(8,128)(2,1)S(1)} %bitcast.20) | data formatting | bytes 3932160
  (4 shorter events, 0.0 us)
Async XLA Ops:
  4.5 4.1 %copy-start = (f32[160,384]{1,0:T(8,128)S(1)}, f32[160,384]{1,0:T(8,128)}, u32[]{:S(2)}) copy-start(f32[160,384]{1,0:T(8,128)} %refs_3_.1) | copy-start | bytes 737284
  4.5 4.1 %copy-start.1 = (f32[64]{0:T(128)S(1)}, f32[64]{0:T(128)}, u32[]{:S(2)}) copy-start(f32[64]{0:T(128)} %param.17) | copy-start | bytes 772
  4.5 4.1 %copy-start.2 = (f32[64]{0:T(128)S(1)}, f32[64]{0:T(128)}, u32[]{:S(2)}) copy-start(f32[64]{0:T(128)} %param.20) | copy-start | bytes 772
  4.5 4.1 %copy-start.3 = (f32[64]{0:T(128)S(1)}, f32[64]{0:T(128)}, u32[]{:S(2)}) copy-start(f32[64]{0:T(128)} %param.23) | copy-start | bytes 772
  88.5 6.6 %copy-start.4 = (bf16[16,160,384]{2,1,0:T(8,128)(2,1)S(1)}, bf16[16,160,384]{2,1,0:T(8,128)(2,1)}, u32[]{:S(2)}) copy-start(bf16[16,160,384]{2,1,0:T(8,128)(2,1)} %get-tuple-element.33) | copy-start | bytes 5898244

commit v2 on v1

--- a/solution.py
+++ b/solution.py
@@ -1,4 +1,5 @@
 import functools
+import math
 
 import jax
 import jax.numpy as jnp
@@ -20,23 +21,26 @@
 
 
 class Plan:
-    def __init__(self, n, tp, mb, own_rows, wq, wl, gains):
+    def __init__(self, n, tp, mb, own_rows, wq, wl, gains, share=0.5):
         self.n, self.tp, self.mb, self.own_rows = n, tp, mb, own_rows
+        self.depth = n * own_rows
         self.m = n // 2
         self.bits = self.m.bit_length() - 1
         self.rp = -(-own_rows // 16) * 16
         self.wq, self.wl, self.gn = wq, wl, gains // n
-        self.nq, self.nl, self.left = wq // LANES, wl // LANES, wl % LANES
-        self.slots = LANES // self.left
-        self.groups = self.rp // 16
-        self.main = self.rp * (self.nq + self.nl)
+        self.nq, self.nl, self.left = wq // LANES, own_rows // LANES, own_rows % LANES
+        self.slot = 1 << max(0, self.left - 1).bit_length()
+        self.slots = LANES // self.slot
+        self.groups = wl // 16
+        self.main = self.rp * self.nq + wl * self.nl
         self.grow = self.main + 16 * (self.groups // self.slots)
         self.rows = self.grow + 16
         self.glane = 64
-        assert wq % LANES == 0 and LANES % self.left == 0 and self.gn <= 64
-        assert self.groups % self.slots * self.left <= self.glane
+        self.per = LANES // self.gn
+        assert wq % LANES == 0 and wl % 16 == 0 and self.left and self.gn <= 64
+        assert LANES % self.gn == 0 and self.groups % self.slots * self.slot <= self.glane
         assert 2 << self.bits == n
-        self.cut = int(self.rows * 0.5) // 16 * 16
+        self.cut = int(self.rows * share) // 16 * 16
         self.halves = ((0, self.cut), (self.cut, self.rows - self.cut))
         first = list(range(self.bits))
         second = first[1:2] + first[:1] + first[2:]
@@ -44,7 +48,13 @@
 
     def leftover(self):
         for g in range(self.groups):
-            yield self.main + 16 * (g // self.slots), self.left * (g % self.slots), 16 * g
+            yield self.main + 16 * (g // self.slots), self.slot * (g % self.slots), 16 * g
+
+    def window(self, block):
+        tile = self.own_rows * block // LANES
+        if self.own_rows * (self.n - 1) // LANES > self.depth // LANES - 2:
+            tile = jnp.minimum(tile, self.depth // LANES - 2)
+        return pl.ds(pl.multiple_of(LANES * tile, LANES), 2 * LANES), self.own_rows * block - LANES * tile
 
     def slots_after(self, half, step):
         done = self.orders[half][: step + 1]
@@ -60,10 +70,10 @@
 def kernel(plan, count, *refs):
     (gq, gl, gg, pq, pl_, pg, fq, fl, fg, sq, sl, sg,
      nq, nl, ng, mq, ml, mg, vq, vl, vg, tq, tl, tg,
-     own_q, own_l, in_q, in_l, in_g, gsum, acc, rbuf, total, stage, norm, ag, agc, tgs,
-     cq_s, cq_r, cl_s, cl_r, cg_s, cg_r, oq, ol, rs_s, rs_r, no_s, no_r, ag_s, ag_r, ac_s, ac_r) = refs
+     in_q, in_l, in_g, gsum, acc, rbuf, total, stage, norm, ag, agc, tgs, tls, lat,
+     cq_s, cq_r, cl_s, cl_r, cg_s, cg_r, rs_s, rs_r, no_s, no_r, ag_s, ag_r, ac_s, ac_r) = refs
     n, m, mb, tp, rp = plan.n, plan.m, plan.mb, plan.tp, plan.rp
-    everyone = n * tp
+    everyone, wl = n * tp, plan.wl
     f, t = lax.axis_index("fsdp"), lax.axis_index("tp")
     core, up = f % 2, f // 2
     me = f * tp + t
@@ -89,6 +99,9 @@
     def theirs(d):
         return 2 * flip(up, d) + 1 - core
 
+    def gain_window(block):
+        return pl.ds(pl.multiple_of(LANES * (block // plan.per), LANES), LANES), plan.gn * (block % plan.per)
+
     def remote(src, dst, send, recv, to):
         return pltpu.make_async_remote_copy(
             src_ref=src, dst_ref=dst, send_sem=send, recv_sem=recv, device_id=to, device_id_type=MESH
@@ -96,14 +109,8 @@
 
     order = sorted(range(1, m), key=lambda d: (not all(d >> o[0] & 1 for o in plan.orders),
                                                not any(d >> o[0] & 1 for o in plan.orders), d)) + [0]
-    local_copies = []
-    for d in order:
-        a = pltpu.make_async_copy(gq.at[:, mine(d)], own_q.at[d], oq.at[d])
-        b = pltpu.make_async_copy(gl.at[:, mine(d)], own_l.at[d], ol.at[d])
-        a.start()
-        b.start()
-        local_copies.append((a, b))
-
+    tls[...] = jnp.zeros(tls.shape, f32)
+    tgs[...] = jnp.zeros(tgs.shape, f32)
     barrier = pltpu.get_barrier_semaphore()
 
     @pl.loop(1, everyone)
@@ -117,7 +124,7 @@
     core_copies = []
     for d in order:
         a = remote(gq.at[:, theirs(d)], in_q.at[d], cq_s.at[d], cq_r.at[d], sibling)
-        b = remote(gl.at[:, theirs(d)], in_l.at[d], cl_s.at[d], cl_r.at[d], sibling)
+        b = remote(gl.at[:, :, plan.window(theirs(d))[0]], in_l.at[d], cl_s.at[d], cl_r.at[d], sibling)
         a.start()
         b.start()
         core_copies.append((a, b))
@@ -135,37 +142,40 @@
             partner(k),
         )
 
-    def gather_sum(refs_, d, lo, hi):
+    def added(terms):
         value = None
-        for ref in refs_:
-            for i in range(mb):
-                term = ref[d, i, :, lo:hi].astype(f32)
-                value = term if value is None else value + term
+        for term in terms:
+            value = term.astype(f32) if value is None else value + term.astype(f32)
         return value
 
     gain_copy.wait()
-    total_gains = None
-    for ref in (gg, in_g):
-        for i in range(mb):
-            term = ref[i].astype(f32)
-            total_gains = term if total_gains is None else total_gains + term
-    gsum[...] = total_gains
+    total_gains = added([ref[i] for ref in (gg, in_g) for i in range(mb)])
+    gsum[...] = jnp.broadcast_to(total_gains, gsum.shape)
 
     for place, d in enumerate(order):
-        for copy in local_copies[place]:
-            copy.wait()
         for copy in core_copies[place]:
             copy.wait()
         for j in range(plan.nq):
-            acc[d, rp * j : rp * (j + 1)] = gather_sum((own_q, in_q), d, LANES * j, LANES * (j + 1))
+            acc[d, rp * j : rp * (j + 1)] = added(
+                [gq[i, mine(d), :, LANES * j : LANES * (j + 1)] for i in range(mb)]
+                + [in_q[d, i, :, LANES * j : LANES * (j + 1)] for i in range(mb)]
+            )
+        acc[d, plan.main : plan.rows] = jnp.zeros((plan.rows - plan.main, LANES), f32)
+        tile, start = plan.window(mine(d))
+        latent = added([gl[i, :, tile] for i in range(mb)] + [in_l[d, i] for i in range(mb)])
+        latent = pltpu.roll(latent, (2 * LANES - start) % (2 * LANES), 1)
         for j in range(plan.nl):
-            lo = rp * (plan.nq + j)
-            acc[d, lo : lo + rp] = gather_sum((own_l, in_l), d, LANES * j, LANES * (j + 1))
-        acc[d, plan.main : plan.rows] = jnp.zeros((plan.rows - plan.main, LANES), f32)
-        last = gather_sum((own_l, in_l), d, LANES * plan.nl, plan.wl)
+            lo = rp * plan.nq + wl * j
+            acc[d, lo : lo + wl] = latent[:, LANES * j : LANES * (j + 1)]
         for row, lane, source in plan.leftover():
-            acc[d, row : row + 16, lane : lane + plan.left] = last[source : source + 16]
-        acc[d, plan.grow : plan.grow + 1, plan.glane : plan.glane + plan.gn] = gsum[pl.ds(mine(d), 1), :]
+            acc[d, row : row + 16, lane : lane + plan.left] = latent[
+                source : source + 16, LANES * plan.nl : LANES * plan.nl + plan.left
+            ]
+        tile, start = gain_window(mine(d))
+        gains = pltpu.roll(gsum[:, tile], (plan.glane - start + LANES) % LANES, 1)
+        acc[d, plan.grow : plan.grow + 1, plan.glane : plan.glane + plan.gn] = gains[
+            0:1, plan.glane : plan.glane + plan.gn
+        ]
         for half in range(2):
             if d >> plan.orders[half][0] & 1:
                 rs_copy(half, 0, d).start()
@@ -224,13 +234,15 @@
         return p - rate * (ratio + decay * p), first_new, second_new
 
     for j in range(plan.nq + plan.nl):
-        params = (pq, fq, sq) if j < plan.nq else (pl_, fl, sl)
-        outs = (nq, mq, vq) if j < plan.nq else (nl, ml, vl)
-        lo = LANES * (j if j < plan.nq else j - plan.nq)
-        values = update(total[rp * j : rp * (j + 1)], *(ref[:, lo : lo + LANES] for ref in params), 0.1)
+        query = j < plan.nq
+        params = (pq, fq, sq) if query else (pl_, fl, sl)
+        outs = (nq, mq, vq) if query else (nl, ml, vl)
+        lane = LANES * (j if query else j - plan.nq)
+        lo, size = (rp * j, rp) if query else (rp * plan.nq + wl * (j - plan.nq), wl)
+        values = update(total[lo : lo + size], *(ref[:, lane : lane + LANES] for ref in params), 0.1)
         for ref, value in zip(outs, values):
-            ref[:, lo : lo + LANES] = value
-        ag[0, rp * j : rp * (j + 1)] = values[0].astype(bf16)
+            ref[:, lane : lane + LANES] = value
+        ag[0, lo : lo + size] = values[0].astype(bf16)
     stage[...] = jnp.zeros(stage.shape, f32)
     for row, lane, source in plan.leftover():
         at = (pl.ds(source, 16), pl.ds(LANES * plan.nl, plan.left))
@@ -268,14 +280,23 @@
         for j in range(plan.nq):
             tq[block, :, LANES * j : LANES * (j + 1)] = ref[d, rp * j : rp * (j + 1)]
         for j in range(plan.nl):
-            lo = rp * (plan.nq + j)
-            tl[block, :, LANES * j : LANES * (j + 1)] = ref[d, lo : lo + rp]
+            lo = rp * plan.nq + wl * j
+            lat[:, LANES * j : LANES * (j + 1)] = ref[d, lo : lo + wl].astype(f32)
+        last = ref[d, plan.main : plan.rows].astype(f32)
         for row, lane, source in plan.leftover():
-            tl[block, source : source + 16, LANES * plan.nl : plan.wl] = ref[
-                d, row : row + 16, lane : lane + plan.left
+            row -= plan.main
+            lat[source : source + 16, LANES * plan.nl : LANES * plan.nl + plan.left] = last[
+                row : row + 16, lane : lane + plan.left
             ]
-        gains = ref[d, plan.grow : plan.grow + 16].astype(f32)
-        tgs[pl.ds(block, 1), :] = gains[0:1, plan.glane : plan.glane + plan.gn]
+        tile, start = plan.window(block)
+        lanes = lax.broadcasted_iota(jnp.int32, lat.shape, 1)
+        inside = (lanes >= start) & (lanes < start + plan.own_rows)
+        tls[:, tile] = jnp.where(inside, pltpu.roll(lat[...], start, 1), tls[:, tile])
+        tile, start = gain_window(block)
+        row = plan.grow - plan.main
+        gains = pltpu.roll(last[row : row + 8], (start - plan.glane + LANES) % LANES, 1)
+        lanes = lax.broadcasted_iota(jnp.int32, gains.shape, 1)
+        tgs[:, tile] = jnp.where((lanes >= start) & (lanes < start + plan.gn), gains, tgs[:, tile])
 
     for half in range(2):
         arrived(half, plan.bits, 0)
@@ -293,7 +314,8 @@
         for half in range(2):
             across(half, d).wait_recv()
         write(agc, d, theirs(d))
-    tg[...] = tgs[...].astype(bf16)
+    tl[...] = tls[...].astype(bf16)
+    tg[...] = tgs[0:1].astype(bf16)
 
     for half in range(2):
         for step in range(plan.bits):
@@ -305,6 +327,16 @@
             across(half, d).wait_send()
 
 
+def hand_over(*refs):
+    count = len(refs) // 2
+    sems = refs[-1]
+    copies = [pltpu.make_async_copy(refs[i], refs[count + i], sems.at[i]) for i in range(count)]
+    for copy in copies:
+        copy.start()
+    for copy in copies:
+        copy.wait()
+
+
 def local(grad_query, grad_latent, grad_gains, *state):
     n, tp = lax.axis_size("fsdp"), lax.axis_size("tp")
     mb, _, depth, wq = grad_query.shape
@@ -313,63 +345,63 @@
     count = depth * (wq + wl) * tp + gains
     extra = plan.rp - plan.own_rows
 
-    def blocks(x):
-        x = x.reshape(mb, n, plan.own_rows, x.shape[3])
-        return jnp.pad(x, ((0, 0), (0, 0), (0, extra), (0, 0))) if extra else x
-
-    def own(x):
-        if x.ndim == 1:
-            return x.reshape(1, plan.gn)
-        return jnp.pad(x, ((0, extra), (0, 0))) if extra else x
-
-    state = [own(x) for x in state]
+    def pad(x):
+        return jnp.pad(x, [(0, 0)] * (x.ndim - 2) + [(0, extra), (0, 0)]) if extra else x
+
+    query = pad(grad_query.reshape(mb, n, plan.own_rows, wq))
+    latent = jnp.swapaxes(grad_latent[:, 0], 1, 2)
+    kept = []
+    for i in range(3):
+        kept += [pad(state[3 * i]), state[3 * i + 1].T, state[3 * i + 2].reshape(1, plan.gn)]
     m, rp = plan.m, plan.rp
     vmem = pl.BlockSpec(memory_space=pltpu.VMEM)
-    anywhere = pl.BlockSpec(memory_space=pl.ANY)
-    shapes = [(rp, wq), (rp, wl), (1, plan.gn)] * 3
+    hbm = pl.BlockSpec(memory_space=pltpu.HBM)
+    out_shape = [
+        jax.ShapeDtypeStruct(s, f32) for s in [(rp, wq), (wl, plan.own_rows), (1, plan.gn)] * 3
+    ] + [jax.ShapeDtypeStruct(s, bf16) for s in [(n, rp, wq), (wl, depth), (1, gains)]]
+    scratch = [
+        pltpu.VMEM((m, mb, rp, wq), bf16),
+        pltpu.VMEM((m, mb, wl, 2 * LANES), bf16),
+        pltpu.VMEM((mb, 1, gains), bf16),
+        pltpu.VMEM((8, gains), f32),
+        pltpu.VMEM((m, plan.rows, LANES), f32),
+        pltpu.VMEM((2 * (m - 1), max(s for _, s in plan.halves), LANES), f32),
+        pltpu.VMEM((plan.rows, LANES), f32),
+        pltpu.VMEM((plan.rows - plan.main, LANES), f32),
+        pltpu.VMEM((n * tp, 8, LANES), f32),
+        pltpu.VMEM((m, plan.rows, LANES), bf16),
+        pltpu.VMEM((m, plan.rows, LANES), bf16),
+        pltpu.VMEM((8, gains), f32),
+        pltpu.VMEM((wl, depth), f32),
+        pltpu.VMEM((wl, 2 * LANES), f32),
+    ]
+    planned = sum(math.prod(x.shape) * x.dtype.itemsize for x in scratch)
     outs = pl.pallas_call(
         functools.partial(kernel, plan, count),
-        out_shape=[jax.ShapeDtypeStruct(s, f32) for s in shapes]
-        + [
-            jax.ShapeDtypeStruct((n, rp, wq), bf16),
-            jax.ShapeDtypeStruct((n, rp, wl), bf16),
-            jax.ShapeDtypeStruct((n, plan.gn), bf16),
-        ],
-        in_specs=[anywhere, anywhere] + [vmem] * 10,
+        out_shape=out_shape,
+        in_specs=[vmem] * 12,
         out_specs=[vmem] * 12,
-        scratch_shapes=[
-            pltpu.VMEM((m, mb, rp, wq), bf16),
-            pltpu.VMEM((m, mb, rp, wl), bf16),
-            pltpu.VMEM((m, mb, rp, wq), bf16),
-            pltpu.VMEM((m, mb, rp, wl), bf16),
-            pltpu.VMEM((mb, n, plan.gn), bf16),
-            pltpu.VMEM((n, plan.gn), f32),
-            pltpu.VMEM((m, plan.rows, LANES), f32),
-            pltpu.VMEM((2 * (m - 1), max(s for _, s in plan.halves), LANES), f32),
-            pltpu.VMEM((plan.rows, LANES), f32),
-            pltpu.VMEM((plan.rows - plan.main, LANES), f32),
-            pltpu.VMEM((n * tp, 8, LANES), f32),
-            pltpu.VMEM((m, plan.rows, LANES), bf16),
-            pltpu.VMEM((m, plan.rows, LANES), bf16),
-            pltpu.VMEM((n, plan.gn), f32),
-        ]
+        scratch_shapes=scratch
         + [
             pltpu.SemaphoreType.DMA((k,))
-            for k in [m] * 4 + [1] * 2 + [m] * 2 + [2 * (m - 1)] * 2 + [n * tp] * 2 + [2 * (m - 1)] * 2 + [2 * m] * 2
+            for k in [m] * 4 + [1] * 2 + [2 * (m - 1)] * 2 + [n * tp] * 2 + [2 * (m - 1)] * 2 + [2 * m] * 2
         ],
         compiler_params=pltpu.CompilerParams(
-            collective_id=0, has_side_effects=True, vmem_limit_bytes=52 * 1024 * 1024
+            collective_id=0, has_side_effects=True, vmem_limit_bytes=planned + (14 << 20)
         ),
-    )(blocks(grad_query), blocks(grad_latent), grad_gains.reshape(mb, n, plan.gn), *state)
+    )(query, latent, grad_gains, *kept)
+    outs = pl.pallas_call(
+        hand_over,
+        out_shape=out_shape,
+        in_specs=[vmem] * 12,
+        out_specs=[hbm] * 12,
+        scratch_shapes=[pltpu.SemaphoreType.DMA((12,))],
+        compiler_params=pltpu.CompilerParams(vmem_limit_bytes=8 << 20),
+    )(*outs)
     result = []
-    for x in outs[:9]:
-        if x.shape[0] == 1:
-            result.append(x.reshape(plan.gn))
-        else:
-            result.append(x[: plan.own_rows] if extra else x)
-    for x in outs[9:11]:
-        result.append(x[:, : plan.own_rows].reshape(depth, x.shape[2]))
-    result.append(outs[11].reshape(gains))
+    for i in range(3):
+        result += [outs[3 * i][: plan.own_rows], outs[3 * i + 1].T, outs[3 * i + 2].reshape(plan.gn)]
+    result += [outs[9][:, : plan.own_rows].reshape(depth, wq), outs[10].T, outs[11].reshape(gains)]
     return tuple(result)
 
 

time: 97 us -> 90.8 us (0.936)
  local copies, waits for them, and re-layouts: 18 us -> 11.7 us
    unnamed x25 -> x23, local copies, waits for them, and re-layouts: 16.5 us -> 11.7 us
    reshape x2 -> x0, local copies, waits for them, and re-layouts: 1.43 us -> none  [the longest x1 0.77 us: local(): grad_gains.reshape(mb, n, plan.gn)]
    pallas_call x1 -> x2, Pallas kernels: 77.7 us -> 77.5 us  [the longest x1 75.4 us: local(): pl.pallas_call(functools.partial(kernel, plan, count), out_shape=out_shap...]
where the time goes in v2:
time: 90.8 us; the launch traced here: 90.4 us
  Pallas kernels  77.5 us (85%)
  local copies, waits for them, and re-layouts  11.7 us (13%)
    pallas_call x1, Pallas kernels, local(): pl.pallas_call(functools.partial(kernel, plan, count), out_shape=out_shap...  75.4 us
    unnamed x23, local copies, waits for them, and re-layouts  11.7 us
    pallas_call x1, Pallas kernels, local(): pl.pallas_call(hand_over, out_shape=out_shape, in_specs=[vmem] * 12, out_...  2.03 us

profile of v2, /device:TPU:0, one launch (start us, length us, event | category | flops | bytes accessed | tf_op | source)
XLA Modules:
  0.0 90.4 jit_solution(7554064302911293062)
XLA Ops:
  0.6 0.7 copy.24.refs_2_
  1.3 0.0 copy-start
  1.3 2.1 %copy-done = bf16[2,1,2560,384]{3,2,1,0:T(8,128)(2,1)S(1)} copy-done((bf16[2,1,2560,384]{3,2,1,0:T(8,128)(2,1)S(1)}, bf16[2,1,2560,384]{3,2,1,0:T(8,128)(2,1)}, u32[]{:S(2)}) %copy-start) | copy-done | bytes 3932184
  3.5 0.0 copy-start.1
  3.5 1.4 %copy-done.1 = bf16[2,1,2560,144]{2,3,1,0:T(8,128)(2,1)S(1)} copy-done((bf16[2,1,2560,144]{2,3,1,0:T(8,128)(2,1)S(1)}, bf16[2,1,2560,144]{2,3,1,0:T(8,128)(2,1)}, u32[]{:S(2)}) %copy-start.1) | copy-done | bytes 1474584
  4.8 0.0 copy-start.2
  4.8 0.9 %copy-done.2 = f32[160,384]{1,0:T(8,128)S(1)} copy-done((f32[160,384]{1,0:T(8,128)S(1)}, f32[160,384]{1,0:T(8,128)}, u32[]{:S(2)}) %copy-start.2) | copy-done | bytes 245784
  5.8 0.0 copy-start.3
  5.8 0.9 %copy-done.3 = f32[160,384]{1,0:T(8,128)S(1)} copy-done((f32[160,384]{1,0:T(8,128)S(1)}, f32[160,384]{1,0:T(8,128)}, u32[]{:S(2)}) %copy-start.3) | copy-done | bytes 245784
  6.7 0.0 copy-start.4
  6.7 0.9 %copy-done.4 = f32[160,384]{1,0:T(8,128)S(1)} copy-done((f32[160,384]{1,0:T(8,128)S(1)}, f32[160,384]{1,0:T(8,128)}, u32[]{:S(2)}) %copy-start.4) | copy-done | bytes 245784
  7.7 0.0 copy-start.5
  7.7 0.9 %copy-done.5 = f32[160,144]{0,1:T(8,128)S(1)} copy-done((f32[160,144]{0,1:T(8,128)S(1)}, f32[160,144]{0,1:T(8,128)}, u32[]{:S(2)}) %copy-start.5) | copy-done | bytes 92184
  8.6 0.0 copy-start.6
  8.6 0.9 %copy-done.6 = f32[160,144]{0,1:T(8,128)S(1)} copy-done((f32[160,144]{0,1:T(8,128)S(1)}, f32[160,144]{0,1:T(8,128)}, u32[]{:S(2)}) %copy-start.6) | copy-done | bytes 92184
  9.5 0.0 copy-start.7
  9.5 0.9 %copy-done.7 = f32[160,144]{0,1:T(8,128)S(1)} copy-done((f32[160,144]{0,1:T(8,128)S(1)}, f32[160,144]{0,1:T(8,128)}, u32[]{:S(2)}) %copy-start.7) | copy-done | bytes 92184
  10.4 0.0 copy-start.8
  10.4 0.7 copy-done.8
  11.0 0.7 copy-done.9
  11.7 0.7 copy-done.10
  12.4 75.4 %shard_map.211 = (f32[160,384]{1,0:T(8,128)S(1)}, f32[144,160]{1,0:T(8,128)S(1)}, f32[1,64]{1,0:T(1,128)S(1)}, f32[160,384]{1,0:T(8,128)S(1)}, f32[144,160]{1,0:...) custom-call(bf16[2,16,160,384]{3,2,1,0:T(8,128)(2,1)S(1)} %bitcast.1, ...), custom_call_target="tpu_custom_call" | custom-call | tf_op jit(solution)/shard_map/pallas_call | solution.py:379
  87.8 2.0 %shard_map.212 = (f32[160,384]{1,0:T(8,128)}, f32[144,160]{1,0:T(8,128)}, f32[1,64]{1,0:T(1,128)}, f32[160,384]{1,0:T(8,128)}, f32[144,160]{1,0:T(8,128)}, /*ind...) custom-call(f32[160,384]{1,0:T(8,128)S(1)} %get-tuple-element.36.ref, ...), custom_call_target="tpu_custom_call" | custom-call | tf_op jit(solution)/shard_map/pallas_call | solution.py:393
  89.8 0.6 reduce
  (2 shorter events, 0.0 us)
Async XLA Ops:
  1.3 2.1 %copy-start = (bf16[2,1,2560,384]{3,2,1,0:T(8,128)(2,1)S(1)}, bf16[2,1,2560,384]{3,2,1,0:T(8,128)(2,1)}, u32[]{:S(2)}) copy-start(bf16[2,1,2560,384]{3,2,1,0:T(8,128)(2,1)} %param.12) | copy-start | bytes 11796484
  3.5 1.4 %copy-start.1 = (bf16[2,1,2560,144]{2,3,1,0:T(8,128)(2,1)S(1)}, bf16[2,1,2560,144]{2,3,1,0:T(8,128)(2,1)}, u32[]{:S(2)}) copy-start(bf16[2,1,2560,144]{2,3,1,0:T(8,128)(2,1)} %param.13) | copy-start | bytes 4423684
  4.8 0.9 %copy-start.2 = (f32[160,384]{1,0:T(8,128)S(1)}, f32[160,384]{1,0:T(8,128)}, u32[]{:S(2)}) copy-start(f32[160,384]{1,0:T(8,128)} %refs_3_.1) | copy-start | bytes 737284
  5.8 0.9 %copy-start.3 = (f32[160,384]{1,0:T(8,128)S(1)}, f32[160,384]{1,0:T(8,128)}, u32[]{:S(2)}) copy-start(f32[160,384]{1,0:T(8,128)} %refs_6_.1) | copy-start | bytes 737284
  6.7 0.9 %copy-start.4 = (f32[160,384]{1,0:T(8,128)S(1)}, f32[160,384]{1,0:T(8,128)}, u32[]{:S(2)}) copy-start(f32[160,384]{1,0:T(8,128)} %refs_9_.1) | copy-start | bytes 737284
  7.7 0.9 %copy-start.5 = (f32[160,144]{0,1:T(8,128)S(1)}, f32[160,144]{0,1:T(8,128)}, u32[]{:S(2)}) copy-start(f32[160,144]{0,1:T(8,128)} %param.16) | copy-start | bytes 276484
  8.6 0.9 %copy-start.6 = (f32[160,144]{0,1:T(8,128)S(1)}, f32[160,144]{0,1:T(8,128)}, u32[]{:S(2)}) copy-start(f32[160,144]{0,1:T(8,128)} %param.19) | copy-start | bytes 276484
  9.5 0.9 %copy-start.7 = (f32[160,144]{0,1:T(8,128)S(1)}, f32[160,144]{0,1:T(8,128)}, u32[]{:S(2)}) copy-start(f32[160,144]{0,1:T(8,128)} %param.22) | copy-start | bytes 276484
  10.4 0.7 copy-start.8
  11.0 0.7 copy-start.9
  11.7 0.7 copy-start.10

commit v3 on v2

--- a/solution.py
+++ b/solution.py
@@ -355,7 +355,7 @@
         kept += [pad(state[3 * i]), state[3 * i + 1].T, state[3 * i + 2].reshape(1, plan.gn)]
     m, rp = plan.m, plan.rp
     vmem = pl.BlockSpec(memory_space=pltpu.VMEM)
-    hbm = pl.BlockSpec(memory_space=pltpu.HBM)
+    anywhere = pl.BlockSpec(memory_space=pl.ANY)
     out_shape = [
         jax.ShapeDtypeStruct(s, f32) for s in [(rp, wq), (wl, plan.own_rows), (1, plan.gn)] * 3
     ] + [jax.ShapeDtypeStruct(s, bf16) for s in [(n, rp, wq), (wl, depth), (1, gains)]]
@@ -387,16 +387,16 @@
             for k in [m] * 4 + [1] * 2 + [2 * (m - 1)] * 2 + [n * tp] * 2 + [2 * (m - 1)] * 2 + [2 * m] * 2
         ],
         compiler_params=pltpu.CompilerParams(
-            collective_id=0, has_side_effects=True, vmem_limit_bytes=planned + (14 << 20)
+            collective_id=0, has_side_effects=True, vmem_limit_bytes=max(planned + (14 << 20), 58 << 20)
         ),
     )(query, latent, grad_gains, *kept)
     outs = pl.pallas_call(
         hand_over,
         out_shape=out_shape,
-        in_specs=[vmem] * 12,
-        out_specs=[hbm] * 12,
+        in_specs=[anywhere] * 12,
+        out_specs=[anywhere] * 12,
         scratch_shapes=[pltpu.SemaphoreType.DMA((12,))],
-        compiler_params=pltpu.CompilerParams(vmem_limit_bytes=8 << 20),
+        compiler_params=pltpu.CompilerParams(vmem_limit_bytes=58 << 20),
     )(*outs)
     result = []
     for i in range(3):

time: 90.8 us -> 203 us (2.24)
  Pallas kernels: 77.5 us -> 199 us
  local copies, waits for them, and re-layouts: 11.7 us -> 1.29 us
    pallas_call x1, Pallas kernels: 2.03 us -> 119 us  [local(): pl.pallas_call(hand_over, out_shape=out_shape, in_specs=[anywhere] * 12,...]
    unnamed x23 -> x1, local copies, waits for them, and re-layouts: 11.7 us -> 1.29 us
    pallas_call x1, Pallas kernels: 75.4 us -> 80.1 us  [local(): pl.pallas_call(functools.partial(kernel, plan, count), out_shape=out_shap...]
where the time goes in v3:
time: 203 us; the launch traced here: 202 us
  Pallas kernels  199 us (98%)
    pallas_call x1, Pallas kernels, local(): pl.pallas_call(hand_over, out_shape=out_shape, in_specs=[anywhere] * 12,...  119 us
    pallas_call x1, Pallas kernels, local(): pl.pallas_call(functools.partial(kernel, plan, count), out_shape=out_shap...  80.1 us

profile of v3, /device:TPU:0, one launch (start us, length us, event | category | flops | bytes accessed | tf_op | source)
XLA Modules:
  0.0 202.4 jit_solution(11259124410090508035)
XLA Ops:
  0.6 1.3 copy.24.refs_2_
  1.9 80.1 %shard_map.211 = (f32[160,384]{1,0:T(8,128)}, f32[144,160]{1,0:T(8,128)}, f32[1,64]{1,0:T(1,128)}, f32[160,384]{1,0:T(8,128)}, f32[144,160]{1,0:T(8,128)}, /*ind...) custom-call(bf16[2,16,160,384]{3,2,1,0:T(8,128)(2,1)} %bitcast.18, ...), custom_call_target="tpu_custom_call" | custom-call | tf_op jit(solution)/shard_map/pallas_call | solution.py:379
  82.0 119.0 %shard_map.212 = (f32[160,384]{1,0:T(8,128)}, f32[144,160]{1,0:T(8,128)}, f32[1,64]{1,0:T(1,128)}, f32[160,384]{1,0:T(8,128)}, f32[144,160]{1,0:T(8,128)}, /*ind...) custom-call(f32[160,384]{1,0:T(8,128)} %get-tuple-element.36.refs_0_, ...), custom_call_target="tpu_custom_call" | custom-call | tf_op jit(solution)/shard_map/pallas_call | solution.py:393
  201.1 1.3 reduce
